TPU v7x, 512 devices: a whole 4x4x16 slice. The times are simulated.
512 devices in a mesh: section: 4 (over x_lo, core), fsdp: 32 (over x_hi, z), tensor: 4 (over y).
Axes of the slice: x: 4 (x_hi: 2, x_lo: 2; x = x_hi * 2 + x_lo), y: 4, z: 16, core: 2. Of those that a mesh axis runs over, the one named last changes fastest.
Arguments:
- entering: bfloat16 [4, 16384, 2048], P('section', 'fsdp', 'tensor'), may hold values from -8 to 8
- w_query: bfloat16 [4, 2048, 4096], P('section', 'fsdp', 'tensor'), may hold values from -0.125 to 0.125
- w_keyval: bfloat16 [4, 2048, 4, 256], P('section', 'fsdp', 'tensor'), may hold values from -0.125 to 0.125
- w_out: bfloat16 [4, 4096, 2048], P('section', 'tensor', 'fsdp'), may hold values from -0.09375 to 0.09375
Outputs:
- leaving: bfloat16 [4, 16384, 2048], P('section', 'fsdp', 'tensor')
All inputs are finite; a program needn't handle non-finite values.
Results may differ from a plain program's by a relative error of at most 0.0055.
Values may be sent and summed in bfloat16 or wider, within the bound.
A program may use at most 64 MiB of HBM per device.

v0:
```python
import math

import jax
import jax.numpy as jnp
from jax import lax
from jax.sharding import PartitionSpec as P

HEAD_DIM = 128


EPSILON = 1e-06
ROPE_BASE = 1000000.0
BEFORE_SHARE = 0.6
AFTER_SHARE = 0.4


def shifted(block, axis, distance):
    devices = range(lax.axis_size(axis))
    route = [((i - distance) % len(devices), i) for i in devices]
    return lax.ppermute(block, axis, route)


def rope_tables(length, width):
    half_width = width // 2
    exponent = jnp.arange(half_width, dtype=jnp.float32) * (2.0 / width)
    inverse = jnp.exp(-exponent * math.log(ROPE_BASE))
    angles = jnp.arange(length, dtype=jnp.float32)[:, None] * inverse[None, :]
    return (jnp.cos(angles)[:, None, :], jnp.sin(angles)[:, None, :])


def head_norm_rope(vectors, cosine, sine):
    meansq = jnp.mean(vectors * vectors, axis=-1, keepdims=True)
    normed = vectors * lax.rsqrt(meansq + EPSILON)
    half_width = vectors.shape[-1] // 2
    first_half = normed[..., :half_width]
    second_half = normed[..., half_width:]
    return jnp.concatenate(
        [first_half * cosine - second_half * sine, second_half * cosine + first_half * sine],
        axis=-1,
    )


def pack_weights(query_shard, keyval_shard, out_shard):
    return jnp.concatenate(
        [query_shard.reshape(1, -1), keyval_shard.reshape(1, -1), out_shard.reshape(1, -1)], axis=1
    )


def body(entering, w_query, w_keyval, w_out):
    owned_pack = pack_weights(w_query, w_keyval, w_out)
    from_lower = shifted(owned_pack, "section", 1)
    from_upper = shifted(owned_pack, "section", -1)
    section_pack = (
        BEFORE_SHARE * from_lower.astype(jnp.float32) + AFTER_SHARE * from_upper.astype(jnp.float32)
    ).astype(jnp.bfloat16)
    query_count = w_query.size
    keyval_count = w_keyval.size
    query_mine = section_pack[:, :query_count].reshape(w_query.shape)
    keyval_mine = section_pack[:, query_count : query_count + keyval_count].reshape(w_keyval.shape)
    out_mine = section_pack[:, query_count + keyval_count :].reshape(w_out.shape)
    own_rows = entering[0]
    own_float = own_rows.astype(jnp.float32)
    full_rows = lax.all_gather(own_rows, "tensor", axis=1, tiled=True).astype(jnp.float32)
    meansq = jnp.mean(full_rows * full_rows, axis=-1, keepdims=True)
    normed = (full_rows * lax.rsqrt(meansq + EPSILON)).astype(jnp.bfloat16)
    length = normed.shape[0]
    query_width = query_mine.shape[2]
    keyval_width = keyval_mine.shape[2] * keyval_mine.shape[3]
    query_piece = lax.all_gather(query_mine, "fsdp", axis=1, tiled=True)
    keyval_piece = lax.all_gather(keyval_mine, "fsdp", axis=1, tiled=True)
    piece_rows = query_piece.shape[1]
    query_sum = jnp.dot(normed, query_piece[0], preferred_element_type=jnp.float32)
    keyval_sum = jnp.dot(
        normed, keyval_piece[0].reshape(piece_rows, -1), preferred_element_type=jnp.float32
    )
    query_heads = query_width // HEAD_DIM
    kv_count = keyval_width // (2 * HEAD_DIM)
    group_size = query_heads // kv_count
    cosine, sine = rope_tables(length, HEAD_DIM)
    queries = head_norm_rope(
        query_sum.reshape(length, kv_count, group_size, HEAD_DIM),
        cosine[:, :, None, :],
        sine[:, :, None, :],
    ).astype(jnp.bfloat16)
    keyval_heads = keyval_sum.reshape(length, kv_count, 2 * HEAD_DIM)
    keys = head_norm_rope(keyval_heads[..., :HEAD_DIM], cosine, sine).astype(jnp.bfloat16)
    values = keyval_heads[..., HEAD_DIM:].astype(jnp.bfloat16)
    positions = jnp.arange(length)
    causal = positions[:, None] >= positions[None, :]
    scale = 1.0 / math.sqrt(HEAD_DIM)

    def one_group(query_slice):
        scores = (
            jnp.einsum("qkd,pkd->kqp", query_slice, keys, preferred_element_type=jnp.float32)
            * scale
        )
        expo = jnp.where(causal[None], jnp.exp(scores - math.sqrt(HEAD_DIM)), 0.0)
        weights = (expo / jnp.sum(expo, axis=-1, keepdims=True)).astype(jnp.bfloat16)
        return jnp.einsum(
            "kqp,pkd->qkd", weights, values, preferred_element_type=jnp.float32
        ).astype(jnp.bfloat16)

    mixed = lax.map(one_group, jnp.moveaxis(queries, 2, 0))
    mixed = jnp.moveaxis(mixed, 0, 2).reshape(length, query_heads * HEAD_DIM)
    partial_terms = jnp.dot(
        mixed,
        lax.all_gather(out_mine, "fsdp", axis=2, tiled=True)[0],
        preferred_element_type=jnp.float32,
    ).astype(jnp.bfloat16)
    summed = lax.psum_scatter(partial_terms, "tensor", scatter_dimension=1, tiled=True).astype(
        jnp.float32
    )
    return (own_float + summed).astype(jnp.bfloat16)[None]


def solution(mesh):
    in_specs = (
        P("section", "fsdp", "tensor"),
        P("section", "fsdp", "tensor"),
        P("section", "fsdp", "tensor", None),
        P("section", "tensor", "fsdp"),
    )
    out_specs = P("section", "fsdp", "tensor")
    return jax.shard_map(body, mesh=mesh, in_specs=in_specs, out_specs=out_specs, check_vma=False)
```

profile of v0, /device:TPU:24, one launch (start us, length us, event | category | flops | bytes accessed | tf_op | source)
XLA Modules:
  0.0 572.0 jit_solution(11576316620218176375)
XLA Ops:
  6.5 1.1 copy.29
  7.9 0.8 copy.30
  8.7 1.1 copy.20
  10.1 0.3 constant_dynamic-update-slice_fusion.1
  10.4 1.9 collective-permute-start
  12.3 3.6 collective-permute-start.1
  16.0 8.2 %collective-permute-done = bf16[1,147456]{1,0:T(2,128)(2,1)S(1)} collective-permute-done((bf16[1,147456]{1,0:T(2,128)(2,1)S(1)}, bf16[1,147456]{1,0:T(2,128)(2,1)S(1)}, u32[]{:S(2)}, u32[]{:S(2)}) %collective-permute-start) | collective-permute-done | bytes 294944 | tf_op jit(solution)/shard_map/ppermute | solution.py:20
  24.2 2.7 collective-permute-done.1
  26.9 1.4 add_convert_fusion.1
  28.5 0.6 reshape.283
  29.2 1.5 slice_reduce_fusion
  30.7 0.7 reshape.281
  31.5 1.0 fusion.29
  32.6 0.8 copy.26
  33.7 23.2 %all-gather.12.cloned.1.call-done = bf16[1,512,2048]{2,1,0:T(8,128)(2,1)} async-done(((bf16[1,512,512]{2,1,0:T(8,128)(2,1)}), bf16[1,512,2048]{2,1,0:T(8,128)(2,1)}) %all-gather.12.cloned.1.call-update) | async-done | bytes 2097168 | tf_op jit(solution)/shard_map/all_gather | solution.py:63
  56.9 2.2 fusion.11
  59.1 146.1 %all-gather.8.cloned.1.call-done = bf16[1,2048,1,256]{3,1,2,0:T(8,128)(2,1)} async-done(((bf16[1,64,1,256]{3,1,2,0:T(8,128)(2,1)}), bf16[1,2048,1,256]{3,1,2,0:T(8,128)(2,1)}) %all-gather.8.cloned.1.call-update) | async-done | bytes 1048592 | tf_op jit(solution)/shard_map/all_gather | solution.py:70
  205.2 2.1 convolution_bitcast_fusion
  207.4 0.6 subtract_convert_fusion.1
  208.2 158.4 %all-gather.6.cloned.1.call-done = bf16[1,2048,1024]{2,1,0:T(8,128)(2,1)} async-done(((bf16[1,64,1024]{2,1,0:T(8,128)(2,1)}), bf16[1,2048,1024]{2,1,0:T(8,128)(2,1)}) %all-gather.6.cloned.1.call-update) | async-done | bytes 4194320 | tf_op jit(solution)/shard_map/all_gather | solution.py:69
  366.6 4.5 fusion.20
  371.2 0.5 copy.31
  371.7 0.6 multiply_reduce_fusion
  372.4 0.6 copy_multiply_fusion
  373.0 0.8 subtract_convert_fusion
  373.8 0.6 maximum_bitcast_fusion
  374.4 0.6 copy-done.2
  375.0 6.8 %while.13 = (s32[]{:T(128)}, bf16[8,512,1,128]{1,3,0,2:T(8,128)(2,1)S(1)}, bf16[8,512,1,128]{3,1,2,0:T(8,128)(2,1)S(1)}, bf16[512,1,128]{2,0,1:T(8,128)(2,1)S(1)}, bf16[512,1,128]{2,0,1:T(8,128)(2,1)S(1)}, /*index=5*/s32[]{:T(128)}) while((s32[]{:T(128)}, bf16[8,512,1,128]{1,3,0,2:T(8,128)(2,1)S(1)}, ...), condition=%wide.region_5.6_spmd.clone, body=%wide.region_3.5_spmd.clone.sunk | while | flops 136117760 | bytes 3149901 | solution.py:103
  375.0 0.3 fusion.38
  375.3 0.4 fusion.39
  375.9 0.3 fusion.38
  376.2 0.4 fusion.39
  376.7 0.3 fusion.38
  377.0 0.4 fusion.39
  377.6 0.3 fusion.38
  377.9 0.4 fusion.39
  378.4 0.3 fusion.38
  378.7 0.4 fusion.39
  379.3 0.3 fusion.38
  379.6 0.4 fusion.39
  380.1 0.3 fusion.38
  380.4 0.4 fusion.39
  381.0 0.3 fusion.38
  381.3 0.4 fusion.39
  381.8 145.8 %all-gather.10.cloned.1.call-done = bf16[1,1024,2048]{1,2,0:T(8,128)(2,1)} async-done(((bf16[1,1024,64]{1,2,0:T(8,128)(2,1)}), bf16[1,1024,2048]{1,2,0:T(8,128)(2,1)}) %all-gather.10.cloned.1.call-update) | async-done | bytes 4194320 | tf_op jit(solution)/shard_map/all_gather | solution.py:107
  527.7 5.9 %fusion.17 = bf16[512,2048]{1,0:T(8,128)(2,1)} fusion(bf16[512,1024]{0,1:T(8,128)(2,1)S(1)} %bitcast.78, bf16[1,1024,2048]{1,2,0:T(8,128)(2,1)} %all-gather.10.cloned.1.call-done), kind=kOutput, calls=%fused_computation.23 | convolution fusion | flops 2148532224 | bytes 7340032 | tf_op jit(solution)/shard_map/dot_general | solution.py:105
  533.6 30.0 %reduce-scatter.2.cloned.1.call-done = bf16[512,512]{1,0:T(8,128)(2,1)} async-done(((bf16[512,2048]{1,0:T(8,128)(2,1)}), bf16[512,512]{1,0:T(8,128)(2,1)}) %reduce-scatter.2.cloned.1.call-update) | async-done | bytes 524304 | tf_op jit(solution)/shard_map/reduce_scatter | solution.py:110
  563.5 2.0 fusion.27
  (48 shorter events, 2.8 us)
Async XLA Ops:
  6.5 50.4 %all-gather.12.cloned.1.call-start = ((), (), s32[]{:S(2)}) async-start(), calls=%async_computation.5 | async-start | bytes 2621440 | tf_op jit(solution)/shard_map/all_gather | solution.py:63
  10.4 13.8 %collective-permute-start = (bf16[1,147456]{1,0:T(2,128)(2,1)S(1)}, bf16[1,147456]{1,0:T(2,128)(2,1)S(1)}, u32[]{:S(2)}, u32[]{:S(2)}) collective-permute-start(bf16[1,147456]{1,0:T(2,128)(2,1)S(1)} %constant_dynamic-update-slice_fusion.1), channel_id=1, source_target_pairs={{384,0},{0,128},{128,256},{256,384},{385,1},{1,129},{129,257},{257... | collective-permute-start | bytes 884744 | tf_op jit(solution)/shard_map/ppermute | solution.py:20
  12.3 14.6 %collective-permute-start.1 = (bf16[1,147456]{1,0:T(2,128)(2,1)S(1)}, bf16[1,147456]{1,0:T(2,128)(2,1)S(1)}, u32[]{:S(2)}, u32[]{:S(2)}) collective-permute-start(bf16[1,147456]{1,0:T(2,128)(2,1)S(1)} %constant_dynamic-update-slice_fusion.1), channel_id=1, source_target_pairs={{128,0},{256,128},{384,256},{0,384},{129,1},{257,129},{385,257},{1... | collective-permute-start | bytes 884744 | tf_op jit(solution)/shard_map/ppermute | solution.py:20
  16.0 189.2 %all-gather.8.cloned.1.call-start = ((), (), s32[]{:S(2)}) async-start(), calls=%async_computation.2 | async-start | bytes 1081344 | tf_op jit(solution)/shard_map/all_gather | solution.py:70
  29.2 337.5 %all-gather.6.cloned.1.call-start = ((), (), s32[]{:S(2)}) async-start(), calls=%async_computation.1 | async-start | bytes 4325376 | tf_op jit(solution)/shard_map/all_gather | solution.py:69
  31.4 496.2 %all-gather.10.cloned.1.call-start = ((), (), s32[]{:S(2)}) async-start(), calls=%async_computation.3 | async-start | bytes 4325376 | tf_op jit(solution)/shard_map/all_gather | solution.py:107
  33.5 530.1 %reduce-scatter.2.cloned.1.call-start = ((), (), s32[]{:S(2)}) async-start(), calls=%async_computation.4 | async-start | bytes 2621440 | tf_op jit(solution)/shard_map/reduce_scatter | solution.py:110
  56.9 148.3 %copy-start.1 = (bf16[1,512,2048]{2,1,0:T(8,128)(2,1)S(1)}, bf16[1,512,2048]{2,1,0:T(8,128)(2,1)}, u32[]{:S(2)}) copy-start(bf16[1,512,2048]{2,1,0:T(8,128)(2,1)} %all-gather.12.cloned.1.call-done) | copy-start | bytes 6291460
  373.8 1.2 copy-start.2
  533.5 30.0 %copy-start = (bf16[1,512,512]{2,1,0:T(8,128)(2,1)S(1)}, bf16[1,512,512]{2,1,0:T(8,128)(2,1)}, u32[]{:S(2)}) copy-start(bf16[1,512,512]{2,1,0:T(8,128)(2,1)} %param.6) | copy-start | bytes 1572868
Sparse Core Ops, SparseCore 0:
  16.1 40.7 all-gather.11
  60.0 145.1 all-gather.7
  208.3 158.2 all-gather.5
  369.6 158.0 all-gather.9
  533.7 29.7 reduce-scatter.1
where the time goes:
time: 575 us; the launch traced here: 572 us
  waiting for transfers between devices  514 us (89%)
  matrix products  18 us (3%)
  between operations  13.4 us (2%)
  local copies, waits for them, and re-layouts  10.2 us (2%)
  other arithmetic  9.86 us (2%)
  starting transfers between devices  5.91 us (1%)
    all_gather x1, waiting for transfers between devices, body(): query_piece = lax.all_gather(query_mine, 'fsdp', axis=1, tiled=True)  158 us
    all_gather x1, waiting for transfers between devices, body(): keyval_piece = lax.all_gather(keyval_mine, 'fsdp', axis=1, tiled=True)  146 us
    all_gather x1, waiting for transfers between devices, body(): lax.all_gather(out_mine, 'fsdp', axis=2, tiled=True)[0]  146 us
    reduce_scatter x1, waiting for transfers between devices, body(): lax.psum_scatter(partial_terms, 'tensor', scatter_dimension=1, tiled=True)  30 us
    all_gather x1, waiting for transfers between devices, body(): lax.all_gather(own_rows, 'tensor', axis=1, tiled=True).astype(jnp.float32)  23.2 us
  transfers between devices with their start and end apart: 7, of which 7 were waited for; matrix products, arithmetic and copies ran while one was open for 5% of the time, Pallas kernels for 0%

commit v1 on v0

v1 whole, which is shorter than its diff:
```python
import math

import jax
import jax.numpy as jnp
import numpy as np
from jax import lax
from jax.experimental import pallas as pl
from jax.experimental.pallas import tpu as pltpu
from jax.sharding import PartitionSpec as P

HEAD_DIM = 128
EPSILON = 1e-06
ROPE_BASE = 1000000.0
BEFORE_SHARE = 0.6
AFTER_SHARE = 0.4
MESH = pl.DeviceIdType.MESH

ZN = 16
SEC = 4
YN = 4
SEQ = 512
FEAT = 512
ROWS = 64
QE = 512
QL = 768
OE = 512
OL = 512
LOG2E = math.log2(math.e)
NT = (((1,), (1,)), ((), ()))


def rope_tables():
    half = HEAD_DIM // 2
    exponent = np.arange(half, dtype=np.float64) * (2.0 / HEAD_DIM)
    angles = np.arange(SEQ, dtype=np.float64)[:, None] * np.exp(-exponent * math.log(ROPE_BASE))[None, :]
    cosine, sine = np.cos(angles), np.sin(angles)
    return (
        np.concatenate([cosine, cosine], axis=1).astype(np.float32),
        np.concatenate([-sine, sine], axis=1).astype(np.float32),
    )


def kernel(
    e_ref, wq_ref, wkv_ref, wo_ref, cos_ref, sin_ref, out_ref,
    ent, nrm, lo_q, hi_q, lo_kv, hi_kv, lo_o, hi_o, ge, gl, oe, ol,
    qs, ks, vs, mx, pb, rb,
    raw_s, raw_r, ya_s, ya_r, zs, zr, xs, xr, ps, pr,
):
    s, f, t = lax.axis_index("section"), lax.axis_index("fsdp"), lax.axis_index("tensor")
    core = lax.rem(s, 2)
    xh = f // ZN
    z = lax.rem(f, ZN)
    xo = 1 - xh
    fpar = xo * ZN + z
    sec_up, sec_dn = lax.rem(s + 1, SEC), lax.rem(s + SEC - 1, SEC)
    sent = []

    def ydev(j):
        return lax.rem(t + j, YN)

    def zat(x, off):
        return x * ZN + lax.rem(z + 2 * ZN + off, ZN)

    def start(copy):
        copy.start()
        sent.append(copy)

    def remote(src, dst, ss, rs, where):
        return pltpu.make_async_remote_copy(
            src_ref=src, dst_ref=dst, send_sem=ss, recv_sem=rs, device_id=where, device_id_type=MESH
        )

    barrier = pltpu.get_barrier_semaphore()
    peers = [
        (sec_up, f, t), (sec_dn, f, t), (s, fpar, t), (s, zat(xh, 1), t), (s, zat(xh, -1), t),
        (s, f, ydev(1)), (s, f, ydev(2)), (s, f, ydev(3)),
    ]
    for where in peers:
        pl.semaphore_signal(barrier, inc=1, device_id=where, device_id_type=MESH)
    pl.semaphore_wait(barrier, len(peers))

    raw = []
    for i, (src, lo, hi) in enumerate(((wkv_ref, lo_kv, hi_kv), (wq_ref, lo_q, hi_q), (wo_ref, lo_o, hi_o))):
        up = remote(src, lo, raw_s.at[i, 0], raw_r.at[i, 0], (sec_up, f, t))
        dn = remote(src, hi, raw_s.at[i, 1], raw_r.at[i, 1], (sec_dn, f, t))
        start(up)
        start(dn)
        raw.append((up, dn))

    yag = []
    for j in (1, 3, 2):
        start(remote(e_ref, ent.at[t], ya_s.at[j], ya_r.at[j], (s, f, ydev(j))))
        src = lax.rem(t + YN - j, YN)
        yag.append(remote(e_ref, ent.at[src], ya_s.at[j], ya_r.at[j], (s, f, ydev(j))))
    ent[pl.ds(t, 1)] = e_ref[...][None]

    def mix(lo, hi):
        return (BEFORE_SHARE * lo.astype(jnp.float32) + AFTER_SHARE * hi.astype(jnp.float32)).astype(jnp.bfloat16)

    streams = ((ge, xh, None), (gl, xh, 0), (ge, xo, None), (oe, xh, None), (ol, xh, 1), (oe, xo, None))

    def zsend(i, d, k):
        buf, x, _ = streams[i]
        b = zat(x, -d * (k - 1))
        c = 0 if d == 1 else 1
        start(remote(buf.at[b], buf.at[b], zs.at[i, c, k - 1], zr.at[i, c, k - 1], (s, zat(xh, d), t)))

    def zwait(i, d, k):
        buf, x, _ = streams[i]
        b = zat(x, -d * k)
        c = 0 if d == 1 else 1
        remote(buf.at[b], buf.at[b], zs.at[i, c, k - 1], zr.at[i, c, k - 1], (s, zat(xh, d), t)).wait_recv()

    sign = 1 - 2 * core

    def zlast(i):
        buf, x, _ = streams[i]
        b = zat(x, -7 * sign)
        start(remote(buf.at[b], buf.at[b], zs.at[i, 0, 7], zr.at[i, 0, 7], (s, zat(xh, sign), t)))

    def zlast_wait(i):
        buf, x, _ = streams[i]
        b = zat(x, 8)
        remote(buf.at[b], buf.at[b], zs.at[i, 0, 7], zr.at[i, 0, 7], (s, zat(xh, sign), t)).wait_recv()

    def xsend(buf, late, off, slot):
        b = zat(xh, off)
        start(remote(buf.at[b], buf.at[b], xs.at[late, slot], xr.at[late, slot], (s, fpar, t)))

    def xwait(buf, late, off, slot):
        b = zat(xo, off)
        remote(buf.at[b], buf.at[b], xs.at[late, slot], xr.at[late, slot], (s, fpar, t)).wait_recv()

    def slot_of(d, k):
        return k if d == 1 else 7 + k

    def forward(i, d, k):
        buf, _, late = streams[i]
        zwait(i, d, k)
        if k < 7:
            zsend(i, d, k + 1)
        if late is not None:
            xsend(buf, late, -d * k, slot_of(d, k))

    def ring_step(ids, k):
        for i in ids:
            if k < 8:
                forward(i, 1, k)
                forward(i, -1, k)
                if k == 7:
                    zlast(i)
            else:
                zlast_wait(i)
                buf, _, late = streams[i]
                if late is not None:
                    xsend(buf, late, 8, 15)

    def late_wait(buf, late):
        xwait(buf, late, 0, 0)
        for k in range(1, 8):
            xwait(buf, late, -k, slot_of(1, k))
            xwait(buf, late, k, slot_of(-1, k))
        xwait(buf, late, 8, 15)

    for up, dn in raw[:2]:
        up.wait_recv()
        dn.wait_recv()
    ge[pl.ds(f, 1), :, 0:256] = mix(lo_kv[...], hi_kv[...])[None]
    ge[pl.ds(f, 1), :, 256:512] = mix(lo_q[:, 0:256], hi_q[:, 0:256])[None]
    gl[pl.ds(f, 1)] = mix(lo_q[:, 256:1024], hi_q[:, 256:1024])[None]
    xsend(ge, 2, 0, 0)
    for i in (0, 1):
        zsend(i, 1, 1)
        zsend(i, -1, 1)
    xsend(gl, 0, 0, 0)
    raw[2][0].wait_recv()
    raw[2][1].wait_recv()
    oe[pl.ds(f, 1)] = mix(lo_o[:, 0:512], hi_o[:, 0:512])[None]
    ol[pl.ds(f, 1)] = mix(lo_o[:, 512:1024], hi_o[:, 512:1024])[None]
    xsend(oe, 2, 0, 1)
    xwait(ge, 2, 0, 0)
    zsend(2, 1, 1)
    zsend(2, -1, 1)

    def normalise():
        @pl.loop(0, 4)
        def _(m):
            rows = pl.ds(pl.multiple_of(m * 128, 128), 128)
            total = jnp.zeros((128, 1), jnp.float32)
            for c in range(YN):
                block = ent[c, rows, :].astype(jnp.float32)
                total = total + jnp.sum(block * block, axis=1, keepdims=True)
            factor = lax.rsqrt(total * (1.0 / (YN * FEAT)) + EPSILON)
            for c in range(YN):
                block = ent[c, rows, :].astype(jnp.float32)
                nrm[rows, c * FEAT : (c + 1) * FEAT] = (block * factor).astype(jnp.bfloat16)

    for k in range(1, 9):
        ring_step((0, 1, 2), k)
        if k == 3:
            for copy in yag:
                copy.wait_recv()
            normalise()
        if k == 7:
            xwait(oe, 2, 0, 1)
            for i in (3, 4, 5):
                zsend(i, 1, 1)
                zsend(i, -1, 1)
    xsend(ol, 1, 0, 0)
    late_wait(gl, 0)

    def rotate(vectors, rows):
        meansq = jnp.mean(vectors * vectors, axis=-1, keepdims=True)
        normed = vectors * lax.rsqrt(meansq + EPSILON)
        turned = normed * cos_ref[rows, :] + pltpu.roll(normed, 64, 1) * sin_ref[rows, :]
        return turned.astype(jnp.bfloat16)

    def project(src, col, rows):
        weight = src[:, :, pl.ds(col, 256)].reshape(2 * ZN * ROWS, 256)
        return jnp.dot(nrm[rows, :], weight, preferred_element_type=jnp.float32)

    @pl.loop(0, 2)
    def _(m):
        rows = pl.ds(pl.multiple_of(m * 256, 256), 256)
        both = project(ge, 0, rows)
        ks[rows, :] = rotate(both[:, :128], rows)
        vs[rows, :] = both[:, 128:].astype(jnp.bfloat16)
        pair = project(ge, 256, rows)
        qs[0, rows, :] = rotate(pair[:, :128], rows)
        qs[1, rows, :] = rotate(pair[:, 128:], rows)

    def late_queries(n):
        @pl.loop(0, 2)
        def _(m):
            rows = pl.ds(pl.multiple_of(m * 256, 256), 256)
            pair = project(gl, n * 256, rows)
            qs[2 + 2 * n, rows, :] = rotate(pair[:, :128], rows)
            qs[3 + 2 * n, rows, :] = rotate(pair[:, 128:], rows)

    mul = LOG2E / math.sqrt(HEAD_DIM)
    sub = LOG2E * math.sqrt(HEAD_DIM)

    def expo(queries, keys, masked):
        scores = lax.dot_general(queries, keys, NT, preferred_element_type=jnp.float32)
        value = jnp.exp2(scores * mul - sub)
        if masked:
            row = lax.broadcasted_iota(jnp.int32, value.shape, 0)
            col = lax.broadcasted_iota(jnp.int32, value.shape, 1)
            value = jnp.where(row >= col, value, 0.0)
        return value

    def attend(h):
        cols = pl.ds(pl.multiple_of(h * 128, 128), 128)
        e = expo(qs[h, 0:256, :], ks[0:256, :], True)
        w = (e * (1.0 / jnp.sum(e, axis=-1, keepdims=True))).astype(jnp.bfloat16)
        mx[0:256, cols] = jnp.dot(w, vs[0:256, :], preferred_element_type=jnp.float32).astype(jnp.bfloat16)
        queries = qs[h, 256:512, :]
        e0 = expo(queries, ks[0:256, :], False)
        e1 = expo(queries, ks[256:512, :], True)
        r = 1.0 / (jnp.sum(e0, axis=-1, keepdims=True) + jnp.sum(e1, axis=-1, keepdims=True))
        w0 = (e0 * r).astype(jnp.bfloat16)
        w1 = (e1 * r).astype(jnp.bfloat16)
        mixed = jnp.dot(w0, vs[0:256, :], preferred_element_type=jnp.float32)
        mixed = mixed + jnp.dot(w1, vs[256:512, :], preferred_element_type=jnp.float32)
        mx[256:512, cols] = mixed.astype(jnp.bfloat16)

    for k in range(1, 9):
        ring_step((3, 4, 5), k)
        if k in (1, 2, 3):
            late_queries(k - 1)

        if k < 5:
            @pl.loop(0, 2)
            def _(j):
                attend(2 * (k - 1) + j)
    late_wait(ol, 1)

    def partial(target, rows):
        first = oe[pl.ds(target * 8, 8)].reshape(FEAT, OE)
        second = ol[pl.ds(target * 8, 8)].reshape(FEAT, OL)
        value = lax.dot_general(mx[rows, 0:OE], first, NT, preferred_element_type=jnp.float32)
        value = value + lax.dot_general(mx[rows, OE:], second, NT, preferred_element_type=jnp.float32)
        return value.astype(jnp.bfloat16)

    for j in (2, 1, 3):
        @pl.loop(0, 2)
        def _(m):
            rows = pl.ds(pl.multiple_of(m * 256, 256), 256)
            pb[j - 1, rows, :] = partial(ydev(j), rows)
        start(remote(pb.at[j - 1], rb.at[j - 1], ps.at[j - 1], pr.at[j - 1], (s, f, ydev(j))))

    @pl.loop(0, 2)
    def _(m):
        rows = pl.ds(pl.multiple_of(m * 256, 256), 256)
        pb[3, rows, :] = partial(t, rows)
    for j in (2, 1, 3):
        remote(pb.at[j - 1], rb.at[j - 1], ps.at[j - 1], pr.at[j - 1], (s, f, ydev(j))).wait_recv()

    @pl.loop(0, 4)
    def _(m):
        rows = pl.ds(pl.multiple_of(m * 128, 128), 128)
        total = pb[3, rows, :].astype(jnp.float32)
        for j in range(3):
            total = total + rb[j, rows, :].astype(jnp.float32)
        out_ref[rows, :] = (e_ref[rows, :].astype(jnp.float32) + total).astype(jnp.bfloat16)

    for copy in sent:
        copy.wait_send()


def body(entering, w_query, w_keyval, w_out):
    bf16, vmem, dma = jnp.bfloat16, pltpu.VMEM, pltpu.SemaphoreType.DMA
    cosine, sine = rope_tables()
    out = pl.pallas_call(
        kernel,
        out_shape=jax.ShapeDtypeStruct((SEQ, FEAT), bf16),
        in_specs=[pl.BlockSpec(memory_space=vmem)] * 6,
        out_specs=pl.BlockSpec(memory_space=vmem),
        scratch_shapes=[
            vmem((YN, SEQ, FEAT), bf16), vmem((SEQ, YN * FEAT), bf16),
            vmem((ROWS, 1024), bf16), vmem((ROWS, 1024), bf16),
            vmem((ROWS, 256), bf16), vmem((ROWS, 256), bf16),
            vmem((ROWS, 1024), bf16), vmem((ROWS, 1024), bf16),
            vmem((2 * ZN, ROWS, QE), bf16), vmem((2 * ZN, ROWS, QL), bf16),
            vmem((2 * ZN, ROWS, OE), bf16), vmem((2 * ZN, ROWS, OL), bf16),
            vmem((8, SEQ, HEAD_DIM), bf16), vmem((SEQ, HEAD_DIM), bf16), vmem((SEQ, HEAD_DIM), bf16),
            vmem((SEQ, 1024), bf16), vmem((4, SEQ, FEAT), bf16), vmem((3, SEQ, FEAT), bf16),
            dma((3, 2)), dma((3, 2)), dma((4,)), dma((4,)), dma((6, 2, 8)), dma((6, 2, 8)),
            dma((3, 16)), dma((3, 16)), dma((3,)), dma((3,)),
        ],
        compiler_params=pltpu.CompilerParams(
            collective_id=0, has_side_effects=True, vmem_limit_bytes=56 * 1024 * 1024
        ),
        name="section",
    )(
        entering[0], w_query[0], w_keyval.reshape(ROWS, 256), jnp.swapaxes(w_out[0], 0, 1),
        jnp.asarray(cosine), jnp.asarray(sine),
    )
    return out[None]


def solution(mesh):
    in_specs = (
        P("section", "fsdp", "tensor"),
        P("section", "fsdp", "tensor"),
        P("section", "fsdp", "tensor", None),
        P("section", "tensor", "fsdp"),
    )
    out_specs = P("section", "fsdp", "tensor")
    return jax.shard_map(body, mesh=mesh, in_specs=in_specs, out_specs=out_specs, check_vma=False)
```

time: 575 us -> 129 us (0.22)
  waiting for transfers between devices: 514 us -> 0 us
  Pallas kernels: 0 us -> 127 us
  matrix products: 18 us -> 0 us
  between operations: 13.4 us -> 0.01 us
  other arithmetic: 9.86 us -> 0 us
  local copies, waits for them, and re-layouts: 10.2 us -> 1.87 us
  starting transfers between devices: 5.91 us -> 0 us
    all_gather x4 -> x0, waiting for transfers between devices: 474 us -> none  [the longest x1 158 us: body(): query_piece = lax.all_gather(query_mine, 'fsdp', axis=1, tiled=True)]
    pallas_call x0 -> x1, Pallas kernels: none -> 127 us  [body(): pl.pallas_call(kernel, out_shape=jax.ShapeDtypeStruct((SEQ, FEAT), bf16),...]
    reduce_scatter x1 -> x0, waiting for transfers between devices: 30 us -> none  [body(): lax.psum_scatter(partial_terms, 'tensor', scatter_dimension=1, tiled=True)]
    dot_general x19 -> x0, matrix products: 18 us -> none  [the longest x1 5.89 us: body(): jnp.dot(mixed, lax.all_gather(out_mine, 'fsdp', axis=2, tiled=True)[0], p...]
    ppermute x2 -> x0, waiting for transfers between devices: 10.9 us -> none  [shifted(): return lax.ppermute(block, axis, route)]
  transfers between devices with their start and end apart: 7 -> 0, of which waited for: 7 -> 0; matrix products, arithmetic and copies ran while one was open for 5% -> 0% of each run, Pallas kernels for 0% -> 0%
where the time goes in v1:
time: 129 us
  Pallas kernels  127 us (98%)
  local copies, waits for them, and re-layouts  1.87 us (1%)
    pallas_call x1, Pallas kernels, body(): pl.pallas_call(kernel, out_shape=jax.ShapeDtypeStruct((SEQ, FEAT), bf16),...  127 us

profile of v1, /device:TPU:24, one launch (start us, length us, event | category | flops | bytes accessed | tf_op | source)
XLA Modules:
  0.0 128.6 jit_solution(9858038578648979196)
XLA Ops:
  0.0 126.7 %section.1 = bf16[512,512]{1,0:T(8,128)(2,1)} custom-call(bf16[512,512]{1,0:T(8,128)(2,1)} %bitcast.8, bf16[64,1024]{1,0:T(8,128)(2,1)} %bitcast.9, bf16[64,256]{1,0:T(8,128)(2,1)} %bitcast.11, bf16[64,1024]{1,0:T(8,128)(2,1)} %bitcast.10, f32[512,128]{1,0:T(8,128)} %constant.4.clone.cos_ref, f32[512,128]{1,0:T(8,128)} %constant.5.clone.sin_ref), custom_call_target="tpu_custom_call" | custom-call | tf_op jit(solution)/shard_map/section/pallas_call | solution.py:314
  126.7 1.9 %copy.8 = bf16[1,512,512]{2,1,0:T(8,128)(2,1)} copy(bf16[1,512,512]{2,1,0:T(8,128)(2,1)} %bitcast.7) | data formatting | bytes 1048576

commit v2 on v1

v2 whole, which is shorter than its diff:
```python
import math

import jax
import jax.numpy as jnp
import numpy as np
from jax import lax
from jax.experimental import pallas as pl
from jax.experimental.pallas import tpu as pltpu
from jax.sharding import PartitionSpec as P

HEAD_DIM = 128
EPSILON = 1e-06
ROPE_BASE = 1000000.0
BEFORE_SHARE = 0.6
AFTER_SHARE = 0.4
MESH = pl.DeviceIdType.MESH

ZN = 16
SEC = 4
YN = 4
SEQ = 512
FEAT = 512
ROWS = 64
QE = 512
QL = 768
OE = 384
OL = 640
HALF = ROWS // 2
LOG2E = math.log2(math.e)
EARLY = {5: (2, 3), 6: (4, 5), 7: (6,)}
NT = (((1,), (1,)), ((), ()))


def rope_tables():
    half = HEAD_DIM // 2
    exponent = np.arange(half, dtype=np.float64) * (2.0 / HEAD_DIM)
    angles = np.arange(SEQ, dtype=np.float64)[:, None] * np.exp(-exponent * math.log(ROPE_BASE))[None, :]
    cosine, sine = np.cos(angles), np.sin(angles)
    tables = np.concatenate([cosine, cosine], axis=1), np.concatenate([-sine, sine], axis=1)
    return np.stack(tables).astype(np.float32)


def kernel(
    e_hbm, wq_hbm, wkv_hbm, wo_hbm, table_hbm, out_ref,
    ent, nrm, table, raw_e, raw_l, raw_o,
    ge, gl, oe, ol, acc, qs, ks, vs, mx, pb, po, rb, rl,
    local, raw_s, raw_r, ya_s, ya_r, zs, zr, xs, xr, xe_s, xe_r, ps, pr, rr,
):
    s, f, t = lax.axis_index("section"), lax.axis_index("fsdp"), lax.axis_index("tensor")
    core = lax.rem(s, 2)
    xh = f // ZN
    z = lax.rem(f, ZN)
    xo = 1 - xh
    fpar = xo * ZN + z
    sec_up, sec_dn = lax.rem(s + 1, SEC), lax.rem(s + SEC - 1, SEC)

    def ydev(j):
        return lax.rem(t + j, YN)

    def zat(x, off):
        return x * ZN + lax.rem(z + 2 * ZN + off, ZN)

    def remote(src, dst, ss, rs, where):
        return pltpu.make_async_remote_copy(
            src_ref=src, dst_ref=dst, send_sem=ss, recv_sem=rs, device_id=where, device_id_type=MESH
        )

    loads = [
        pltpu.make_async_copy(e_hbm, ent.at[t], local.at[0]),
        pltpu.make_async_copy(table_hbm, table, local.at[1]),
    ]
    for copy in loads:
        copy.start()

    barrier = pltpu.get_barrier_semaphore()
    peers = [
        (sec_up, f, t), (sec_dn, f, t), (sec_up, fpar, t), (sec_dn, fpar, t), (s, fpar, t), (s, zat(xh, 1), t), (s, zat(xh, -1), t),
        (s, f, ydev(1)), (s, f, ydev(2)), (s, f, ydev(3)),
    ]
    for where in peers:
        pl.semaphore_signal(barrier, inc=1, device_id=where, device_id_type=MESH)
    pl.semaphore_wait(barrier, len(peers))

    def put(src, dst, slot, where):
        remote(src, dst, raw_s.at[0], raw_r.at[slot], where).start()

    for side, section in ((0, sec_up), (1, sec_dn)):
        for away, other in ((0, f), (1, fpar)):
            dst = raw_e.at[2 * away + side]
            put(wkv_hbm, dst.at[:, pl.ds(0, 256)], 2 * away + side, (section, other, t))
            put(wq_hbm.at[:, pl.ds(0, 256)], dst.at[:, pl.ds(256, 256)], 2 * away + side, (section, other, t))
    for side, section in ((0, sec_up), (1, sec_dn)):
        put(wq_hbm.at[:, pl.ds(256, 768)], raw_l.at[side], 4 + side, (section, f, t))

    yin = []
    for j in (1, 3, 2):
        remote(e_hbm, ent.at[t], ya_s.at[0], ya_r.at[j - 1], (s, f, ydev(j))).start()
        src = lax.rem(t + YN - j, YN)
        yin.append(remote(e_hbm, ent.at[src], ya_s.at[0], ya_r.at[j - 1], (s, f, ydev(j))))
    for side, section in ((0, sec_up), (1, sec_dn)):
        put(wo_hbm, raw_o.at[side], 6 + side, (section, f, t))

    def mix(lo, hi):
        return (BEFORE_SHARE * lo.astype(jnp.float32) + AFTER_SHARE * hi.astype(jnp.float32)).astype(jnp.bfloat16)

    streams = (
        (ge, xh, None, 0, ROWS), (gl, xh, 0, 0, ROWS), (ge, xo, None, 0, ROWS),
        (oe, xh, None, 0, ROWS), (ol, xh, 1, 0, HALF), (oe, xo, None, 0, ROWS), (ol, xh, 1, HALF, HALF),
    )

    def zcopy(i, b, r, d):
        buf, _, _, row, rows = streams[i]
        block = buf.at[b, pl.ds(row, rows)]
        return remote(block, block, zs.at[i], zr.at[i, r], (s, zat(xh, d), t))

    def zslot(d, k):
        return k - 1 if d == 1 else 6 + k

    def zsend(i, d, k):
        zcopy(i, zat(streams[i][1], -d * (k - 1)), zslot(d, k), d).start()

    sign = 1 - 2 * core

    def xsend(i, off, slot):
        buf, _, late, row, rows = streams[i]
        block = buf.at[zat(xh, off), pl.ds(row, rows)]
        remote(block, block, xs.at[late], xr.at[late, slot], (s, fpar, t)).start()

    def xwait(late, slot):
        buf = (gl, ol)[late]
        both = buf.at[pl.ds(0, 2 if 0 < slot < 8 else 1)]
        remote(both, both, xs.at[late], xr.at[late, slot], (s, fpar, t)).wait_recv()

    def forward(i, k):
        x, late = streams[i][1:3]
        if k == 8:
            zcopy(i, zat(x, 8), 14, sign).wait_recv()
            if late is not None:
                xsend(i, 8, 8)
            return
        for d in (1, -1):
            zcopy(i, zat(x, -d * k), zslot(d, k), d).wait_recv()
            if k < 7:
                zsend(i, d, k + 1)
            if late is not None:
                xsend(i, -d * k, k)
        if k == 7:
            zcopy(i, zat(x, -7 * sign), 14, sign).start()

    def pair_of(k):
        far = lax.rem(z + k, 2)
        return lax.rem((z + 2 * ZN + far * (k - 1) - (1 - far) * k) // 2, ZN // 2)

    def arrived(dst, slot):
        remote(dst, dst, raw_s.at[0], raw_r.at[slot], (s, fpar, t)).wait_recv()

    for away, stream in ((0, 0), (1, 2)):
        arrived(raw_e.at[2 * away], 2 * away)
        arrived(raw_e.at[2 * away + 1], 2 * away + 1)
        ge[pl.ds((f, fpar)[away], 1)] = mix(raw_e[2 * away], raw_e[2 * away + 1])[None]
        zsend(stream, 1, 1)
        zsend(stream, -1, 1)
    for side in (0, 1):
        arrived(raw_l.at[side], 4 + side)
    gl[pl.ds(f, 1)] = mix(raw_l[0], raw_l[1])[None]
    zsend(1, 1, 1)
    zsend(1, -1, 1)
    xsend(1, 0, 0)
    for side in (0, 1):
        arrived(raw_o.at[side], 6 + side)
    oe[pl.ds(f, 1)] = mix(raw_o[0, :, 0:OE], raw_o[1, :, 0:OE])[None]
    ol[pl.ds(f, 1)] = mix(raw_o[0, :, OE:], raw_o[1, :, OE:])[None]
    early_o = remote(oe.at[f], oe.at[f], xe_s.at[0], xe_r.at[0], (s, fpar, t))
    early_o.start()

    def normalise():
        @pl.loop(0, 4)
        def _(m):
            rows = pl.ds(pl.multiple_of(m * 128, 128), 128)
            total = jnp.zeros((128, 1), jnp.float32)
            for c in range(YN):
                block = ent[c, rows, :].astype(jnp.float32)
                total = total + jnp.sum(block * block, axis=1, keepdims=True)
            factor = lax.rsqrt(total * (1.0 / (YN * FEAT)) + EPSILON)
            for c in range(YN):
                value = (ent[c, rows, :].astype(jnp.float32) * factor).astype(jnp.bfloat16)
                for i in range(4):
                    nrm[4 * c + i, rows, :] = value[:, 128 * i : 128 * i + 128]

    def accumulate(k, buf, base, width):
        pair = pair_of(k)

        @pl.loop(0, 2)
        def _(m):
            rows = pl.ds(pl.multiple_of(m * 256, 256), 256)
            left = jnp.concatenate([nrm[xh * 8 + pair, rows, :], nrm[xo * 8 + pair, rows, :]], axis=1)
            for col in range(0, width, 256):
                weight = jnp.concatenate(
                    [
                        buf[pl.ds(xh * ZN + 2 * pair, 2), :, col : col + 256].reshape(128, 256),
                        buf[pl.ds(xo * ZN + 2 * pair, 2), :, col : col + 256].reshape(128, 256),
                    ],
                    axis=0,
                )
                value = jnp.dot(left, weight, preferred_element_type=jnp.float32)
                at = slice(base + col, base + col + 256)
                if k > 1:
                    value = value + acc[rows, at]
                acc[rows, at] = value

    def accumulate_late(k):
        if k == 1:
            xwait(0, 0)
        xwait(0, k)
        accumulate(k, gl, QE, QL)

    def rotate(vectors, rows):
        meansq = jnp.mean(vectors * vectors, axis=-1, keepdims=True)
        normed = vectors * lax.rsqrt(meansq + EPSILON)
        turned = normed * table[0, rows, :] + pltpu.roll(normed, 64, 1) * table[1, rows, :]
        return turned.astype(jnp.bfloat16)

    def halves(step):
        @pl.loop(0, 4)
        def _(m):
            step(pl.ds(pl.multiple_of(m * 128, 128), 128))

    def finish_early(rows):
        ks[rows, :] = rotate(acc[rows, 0:128], rows)
        vs[rows, :] = acc[rows, 128:256].astype(jnp.bfloat16)
        qs[0, rows, :] = rotate(acc[rows, 256:384], rows)
        qs[1, rows, :] = rotate(acc[rows, 384:512], rows)

    def finish_late(rows):
        for h in range(2, 8):
            qs[h, rows, :] = rotate(acc[rows, QE + 128 * (h - 2) : QE + 128 * (h - 1)], rows)

    mul = LOG2E / math.sqrt(HEAD_DIM)
    sub = LOG2E * math.sqrt(HEAD_DIM)

    def expo(queries, keys, masked):
        scores = lax.dot_general(queries, keys, NT, preferred_element_type=jnp.float32)
        value = jnp.exp2(scores * mul - sub)
        if masked:
            row = lax.broadcasted_iota(jnp.int32, value.shape, 0)
            col = lax.broadcasted_iota(jnp.int32, value.shape, 1)
            value = jnp.where(row >= col, value, 0.0)
        return value

    def attend(h):
        cols = pl.ds(pl.multiple_of(h * 128, 128), 128)
        e = expo(qs[h, 0:256, :], ks[0:256, :], True)
        w = (e * (1.0 / jnp.sum(e, axis=-1, keepdims=True))).astype(jnp.bfloat16)
        mx[0:256, cols] = jnp.dot(w, vs[0:256, :], preferred_element_type=jnp.float32).astype(jnp.bfloat16)
        queries = qs[h, 256:512, :]
        e0 = expo(queries, ks[0:256, :], False)
        e1 = expo(queries, ks[256:512, :], True)
        r = 1.0 / (jnp.sum(e0, axis=-1, keepdims=True) + jnp.sum(e1, axis=-1, keepdims=True))
        w0 = (e0 * r).astype(jnp.bfloat16)
        w1 = (e1 * r).astype(jnp.bfloat16)
        mixed = jnp.dot(w0, vs[0:256, :], preferred_element_type=jnp.float32)
        mixed = mixed + jnp.dot(w1, vs[256:512, :], preferred_element_type=jnp.float32)
        mx[256:512, cols] = mixed.astype(jnp.bfloat16)

    def to_owner(k, slot, quarter, owner):
        j = lax.rem(owner + YN - t, YN) - 1
        remote(pb.at[slot], rb.at[j, quarter], ps.at[0], pr.at[j, quarter], (s, f, owner)).start()

    def partial(k):
        if k == 1:
            xwait(1, 0)
        xwait(1, k)
        pair = pair_of(k)
        quarter = lax.rem(pair, 4)

        @pl.loop(0, 2)
        def _(x):
            owner = 2 * x + pair // 4
            b = pl.ds(x * ZN + 2 * pair, 2)
            slot = 2 * (k - 1) + x
            first = oe[b].reshape(128, OE)
            second = ol[b].reshape(128, OL)
            value = lax.dot_general(mx[:, 0:OE], first, NT, preferred_element_type=jnp.float32)
            value = value + lax.dot_general(mx[:, OE:], second, NT, preferred_element_type=jnp.float32)
            value = value.astype(jnp.bfloat16)

            @pl.when(owner == t)
            def _():
                po[pl.ds(quarter, 1)] = value[None]

            @pl.when(owner != t)
            def _():
                pb[pl.ds(slot, 1)] = value[None]
                if k == 8:
                    to_owner(k, slot, quarter, owner)

            if k < 8:
                @pl.when(owner == ydev(2))
                def _():
                    for side in (0, 1):
                        half = pb.at[slot, pl.ds(256 * side, 256)]
                        remote(half, rl.at[k - 1, side], ps.at[0], rr.at[k - 1, side], (s, f, ydev(1 + 2 * side))).start()

    def relay(k):
        pair = pair_of(k)

        @pl.when(pair // 4 != lax.rem(t, 2))
        def _():
            for side in (0, 1):
                owner = ydev(1 + 2 * side)
                slot = 2 * (k - 1) + owner // 2
                dst = rl.at[k - 1, side]
                remote(dst, dst, ps.at[0], rr.at[k - 1, side], (s, f, owner)).wait_recv()
                rows = slice(256 * side, 256 * side + 256)
                total = pb[slot, rows, :].astype(jnp.float32) + rl[k - 1, side].astype(jnp.float32)
                pb[pl.ds(slot, 1), rows, :] = total.astype(jnp.bfloat16)[None]
                to_owner(k, slot, lax.rem(pair, 4), owner)

    for k in range(1, 8):
        for i in (0, 2):
            forward(i, k)
        if k > 4:
            accumulate(EARLY[k][0], ge, 0, QE)
        forward(1, k)
        if k == 7:
            early_o.wait_recv()
            for i in (3, 4, 6, 5):
                zsend(i, 1, 1)
                zsend(i, -1, 1)
            xsend(4, 0, 0)
            xsend(6, 0, 0)
        if k == 4:
            loads[0].wait()
            for copy in yin:
                copy.wait_recv()
            normalise()
            accumulate(1, ge, 0, QE)
            accumulate_late(1)
        if k > 4:
            accumulate_late(EARLY[k][0])
            for i in EARLY[k][1:]:
                accumulate(i, ge, 0, QE)
                accumulate_late(i)

    forward(0, 8)
    forward(2, 8)
    accumulate(7, ge, 0, QE)
    forward(1, 8)
    forward(3, 1)
    accumulate_late(7)
    accumulate(8, ge, 0, QE)
    loads[1].wait()
    halves(finish_early)
    forward(4, 1)
    forward(6, 1)
    attend(0)
    forward(5, 1)
    attend(1)
    forward(3, 2)
    accumulate_late(8)
    halves(finish_late)
    forward(4, 2)
    forward(6, 2)
    attend(2)
    forward(5, 2)
    attend(3)
    forward(3, 3)
    attend(4)
    attend(5)
    forward(4, 3)
    attend(6)
    forward(6, 3)
    forward(5, 3)
    attend(7)
    forward(3, 4)
    partial(1)
    forward(4, 4)
    forward(6, 4)
    forward(5, 4)
    partial(2)
    for k in range(5, 9):
        forward(3, k)
        forward(4, k)
        relay(k - 4)
        forward(6, k)
        forward(5, k)
        partial(k - 2)
    relay(5)
    partial(7)
    relay(6)
    partial(8)
    relay(7)

    for k in range(1, 9):
        pair = pair_of(k)
        quarter = lax.rem(pair, 4)

        @pl.when(pair // 4 == lax.rem(t, 2))
        def _():
            sources = (0, 2) if k < 8 else (0, 2, 1)
            for j in sources:
                dst = rb.at[j, quarter]
                remote(dst, dst, ps.at[0], pr.at[j, quarter], (s, f, ydev(1))).wait_recv()
            cols = pl.ds(pl.multiple_of(quarter * 128, 128), 128)
            total = po[quarter].astype(jnp.float32)
            for j in sources:
                total = total + rb[j, quarter].astype(jnp.float32)
            out_ref[:, cols] = (ent[t, :, cols].astype(jnp.float32) + total).astype(jnp.bfloat16)

    def left(ref, sem):
        remote(ref, ref, sem, raw_r.at[0], (s, fpar, t)).wait_send()

    left(ge.at[pl.ds(0, 11)], raw_s.at[0])
    left(ent.at[pl.ds(0, 3)], ya_s.at[0])
    early_o.wait_send()
    for i, (buf, _, _, row, rows) in enumerate(streams):
        left(buf.at[pl.ds(0, 15), pl.ds(row, rows)], zs.at[i])
    for late, buf in enumerate((gl, ol)):
        left(buf.at[pl.ds(0, 16)], xs.at[late])
    left(pb.at[pl.ds(0, 12)], ps.at[0])


def body(entering, w_query, w_keyval, w_out):
    bf16, f32, vmem, dma = jnp.bfloat16, jnp.float32, pltpu.VMEM, pltpu.SemaphoreType.DMA
    operands = (
        entering[0], w_query[0], w_keyval.reshape(ROWS, 256), jnp.swapaxes(w_out[0], 0, 1), jnp.asarray(rope_tables())
    )
    out = pl.pallas_call(
        kernel,
        out_shape=jax.ShapeDtypeStruct((SEQ, FEAT), bf16),
        in_specs=[pl.BlockSpec(memory_space=pl.ANY)] * len(operands),
        out_specs=pl.BlockSpec(memory_space=vmem),
        scratch_shapes=[
            vmem((YN, SEQ, FEAT), bf16), vmem((16, SEQ, 128), bf16), vmem((2, SEQ, HEAD_DIM), f32),
            vmem((4, ROWS, QE), bf16), vmem((2, ROWS, QL), bf16), vmem((2, ROWS, OE + OL), bf16),
            vmem((2 * ZN, ROWS, QE), bf16), vmem((2 * ZN, ROWS, QL), bf16),
            vmem((2 * ZN, ROWS, OE), bf16), vmem((2 * ZN, ROWS, OL), bf16),
            vmem((SEQ, QE + QL), f32),
            vmem((8, SEQ, HEAD_DIM), bf16), vmem((SEQ, HEAD_DIM), bf16), vmem((SEQ, HEAD_DIM), bf16),
            vmem((SEQ, OE + OL), bf16), vmem((16, SEQ, 128), bf16), vmem((4, SEQ, 128), bf16),
            vmem((3, 4, SEQ, 128), bf16), vmem((7, 2, 256, 128), bf16),
            dma((2,)), dma((1,)), dma((8,)), dma((1,)), dma((3,)), dma((7,)), dma((7, 15)),
            dma((2,)), dma((2, 9)), dma((1,)), dma((1,)), dma((1,)), dma((3, 4)), dma((7, 2)),
        ],
        compiler_params=pltpu.CompilerParams(
            collective_id=0, has_side_effects=True, vmem_limit_bytes=40 * 1024 * 1024
        ),
        name="section",
    )(*(pltpu.with_memory_space_constraint(value, pltpu.HBM) for value in operands))
    return out[None]


def solution(mesh):
    in_specs = (
        P("section", "fsdp", "tensor"),
        P("section", "fsdp", "tensor"),
        P("section", "fsdp", "tensor", None),
        P("section", "tensor", "fsdp"),
    )
    out_specs = P("section", "fsdp", "tensor")
    return jax.shard_map(body, mesh=mesh, in_specs=in_specs, out_specs=out_specs, check_vma=False)
```

time: 129 us -> 108 us (0.84); the launches traced: 129 us -> 106 us
  Pallas kernels: 127 us -> 105 us
    pallas_call x1, Pallas kernels: 127 us -> 105 us  [body(): pl.pallas_call(kernel, out_shape=jax.ShapeDtypeStruct((SEQ, FEAT), bf16),...]
where the time goes in v2:
time: 108 us; the launch traced here: 106 us
  Pallas kernels  105 us (97%)
    pallas_call x1, Pallas kernels, body(): pl.pallas_call(kernel, out_shape=jax.ShapeDtypeStruct((SEQ, FEAT), bf16),...  105 us

profile of v2, /device:TPU:24, one launch (start us, length us, event | category | flops | bytes accessed | tf_op | source)
XLA Modules:
  0.0 106.2 jit_solution(14917853750681207162)
XLA Ops:
  0.0 105.4 %section.1 = bf16[512,512]{1,0:T(8,128)(2,1)S(1)} custom-call(bf16[512,512]{1,0:T(8,128)(2,1)} %bitcast.8, bf16[64,1024]{1,0:T(8,128)(2,1)} %bitcast.9, bf16[64,256]{1,0:T(8,128)(2,1)} %bitcast.11, bf16[64,1024]{1,0:T(8,128)(2,1)} %bitcast.10, f32[2,512,128]{2,1,0:T(8,128)} %constant.2.clone.table_hbm), custom_call_target="tpu_custom_call" | custom-call | tf_op jit(solution)/shard_map/section/pallas_call | solution.py:428
  105.4 0.8 copy.7

commit v3 on v2

--- a/solution.py
+++ b/solution.py
@@ -14,6 +14,7 @@
 BEFORE_SHARE = 0.6
 AFTER_SHARE = 0.4
 MESH = pl.DeviceIdType.MESH
+RECV = (0, 1, 2, 0, 1, 2, 3)
 
 ZN = 16
 SEC = 4
@@ -84,8 +85,8 @@
     def put(src, dst, slot, where):
         remote(src, dst, raw_s.at[0], raw_r.at[slot], where).start()
 
-    for side, section in ((0, sec_up), (1, sec_dn)):
-        for away, other in ((0, f), (1, fpar)):
+    for away, other in ((0, f), (1, fpar)):
+        for side, section in ((0, sec_up), (1, sec_dn)):
             dst = raw_e.at[2 * away + side]
             put(wkv_hbm, dst.at[:, pl.ds(0, 256)], 2 * away + side, (section, other, t))
             put(wq_hbm.at[:, pl.ds(0, 256)], dst.at[:, pl.ds(256, 256)], 2 * away + side, (section, other, t))
@@ -111,7 +112,7 @@
     def zcopy(i, b, r, d):
         buf, _, _, row, rows = streams[i]
         block = buf.at[b, pl.ds(row, rows)]
-        return remote(block, block, zs.at[i], zr.at[i, r], (s, zat(xh, d), t))
+        return remote(block, block, zs.at[i], zr.at[RECV[i], r], (s, zat(xh, d), t))
 
     def zslot(d, k):
         return k - 1 if d == 1 else 6 + k
@@ -131,7 +132,11 @@
         both = buf.at[pl.ds(0, 2 if 0 < slot < 8 else 1)]
         remote(both, both, xs.at[late], xr.at[late, slot], (s, fpar, t)).wait_recv()
 
-    def forward(i, k):
+    def cross(i, k):
+        for d in (1, -1):
+            xsend(i, -d * k, k)
+
+    def forward(i, k, crossing=True):
         x, late = streams[i][1:3]
         if k == 8:
             zcopy(i, zat(x, 8), 14, sign).wait_recv()
@@ -142,7 +147,7 @@
             zcopy(i, zat(x, -d * k), zslot(d, k), d).wait_recv()
             if k < 7:
                 zsend(i, d, k + 1)
-            if late is not None:
+            if late is not None and crossing:
                 xsend(i, -d * k, k)
         if k == 7:
             zcopy(i, zat(x, -7 * sign), 14, sign).start()
@@ -231,9 +236,12 @@
         qs[0, rows, :] = rotate(acc[rows, 256:384], rows)
         qs[1, rows, :] = rotate(acc[rows, 384:512], rows)
 
-    def finish_late(rows):
-        for h in range(2, 8):
-            qs[h, rows, :] = rotate(acc[rows, QE + 128 * (h - 2) : QE + 128 * (h - 1)], rows)
+    def finish_late(heads):
+        def step(rows):
+            for h in heads:
+                qs[h, rows, :] = rotate(acc[rows, QE + 128 * (h - 2) : QE + 128 * (h - 1)], rows)
+
+        halves(step)
 
     mul = LOG2E / math.sqrt(HEAD_DIM)
     sub = LOG2E * math.sqrt(HEAD_DIM)
@@ -248,19 +256,17 @@
         return value
 
     def attend(h):
-        cols = pl.ds(pl.multiple_of(h * 128, 128), 128)
+        cols = slice(h * 128, h * 128 + 128)
         e = expo(qs[h, 0:256, :], ks[0:256, :], True)
-        w = (e * (1.0 / jnp.sum(e, axis=-1, keepdims=True))).astype(jnp.bfloat16)
-        mx[0:256, cols] = jnp.dot(w, vs[0:256, :], preferred_element_type=jnp.float32).astype(jnp.bfloat16)
+        mixed = jnp.dot(e.astype(jnp.bfloat16), vs[0:256, :], preferred_element_type=jnp.float32)
+        mx[0:256, cols] = (mixed * (1.0 / jnp.sum(e, axis=-1, keepdims=True))).astype(jnp.bfloat16)
         queries = qs[h, 256:512, :]
         e0 = expo(queries, ks[0:256, :], False)
         e1 = expo(queries, ks[256:512, :], True)
+        mixed = jnp.dot(e0.astype(jnp.bfloat16), vs[0:256, :], preferred_element_type=jnp.float32)
+        mixed = mixed + jnp.dot(e1.astype(jnp.bfloat16), vs[256:512, :], preferred_element_type=jnp.float32)
         r = 1.0 / (jnp.sum(e0, axis=-1, keepdims=True) + jnp.sum(e1, axis=-1, keepdims=True))
-        w0 = (e0 * r).astype(jnp.bfloat16)
-        w1 = (e1 * r).astype(jnp.bfloat16)
-        mixed = jnp.dot(w0, vs[0:256, :], preferred_element_type=jnp.float32)
-        mixed = mixed + jnp.dot(w1, vs[256:512, :], preferred_element_type=jnp.float32)
-        mx[256:512, cols] = mixed.astype(jnp.bfloat16)
+        mx[256:512, cols] = (mixed * r).astype(jnp.bfloat16)
 
     def to_owner(k, slot, quarter, owner):
         j = lax.rem(owner + YN - t, YN) - 1
@@ -273,16 +279,16 @@
         pair = pair_of(k)
         quarter = lax.rem(pair, 4)
 
-        @pl.loop(0, 2)
-        def _(x):
+        def weights(buf, width):
+            return jnp.concatenate([buf[pl.ds(x * ZN + 2 * pair, 2)].reshape(128, width) for x in (0, 1)], axis=0)
+
+        both = lax.dot_general(mx[:, 0:OE], weights(oe, OE), NT, preferred_element_type=jnp.float32)
+        both = both + lax.dot_general(mx[:, OE:], weights(ol, OL), NT, preferred_element_type=jnp.float32)
+        both = both.astype(jnp.bfloat16)
+        for x in (0, 1):
             owner = 2 * x + pair // 4
-            b = pl.ds(x * ZN + 2 * pair, 2)
             slot = 2 * (k - 1) + x
-            first = oe[b].reshape(128, OE)
-            second = ol[b].reshape(128, OL)
-            value = lax.dot_general(mx[:, 0:OE], first, NT, preferred_element_type=jnp.float32)
-            value = value + lax.dot_general(mx[:, OE:], second, NT, preferred_element_type=jnp.float32)
-            value = value.astype(jnp.bfloat16)
+            value = both[:, 128 * x : 128 * x + 128]
 
             @pl.when(owner == t)
             def _():
@@ -290,7 +296,7 @@
 
             @pl.when(owner != t)
             def _():
-                pb[pl.ds(slot, 1)] = value[None]
+                pb[slot] = value
                 if k == 8:
                     to_owner(k, slot, quarter, owner)
 
@@ -322,13 +328,11 @@
         if k > 4:
             accumulate(EARLY[k][0], ge, 0, QE)
         forward(1, k)
-        if k == 7:
+        if k == 6:
             early_o.wait_recv()
             for i in (3, 4, 6, 5):
                 zsend(i, 1, 1)
                 zsend(i, -1, 1)
-            xsend(4, 0, 0)
-            xsend(6, 0, 0)
         if k == 4:
             loads[0].wait()
             for copy in yin:
@@ -342,49 +346,65 @@
                 accumulate(i, ge, 0, QE)
                 accumulate_late(i)
 
+    forward(3, 1)
+    forward(4, 1, crossing=False)
+    forward(6, 1, crossing=False)
     forward(0, 8)
+    forward(5, 1)
     forward(2, 8)
     accumulate(7, ge, 0, QE)
     forward(1, 8)
-    forward(3, 1)
-    accumulate_late(7)
+    for i in (4, 6):
+        xsend(i, 0, 0)
+        cross(i, 1)
     accumulate(8, ge, 0, QE)
     loads[1].wait()
     halves(finish_early)
-    forward(4, 1)
-    forward(6, 1)
+    accumulate_late(7)
     attend(0)
-    forward(5, 1)
+    forward(3, 2)
     attend(1)
-    forward(3, 2)
-    accumulate_late(8)
-    halves(finish_late)
     forward(4, 2)
     forward(6, 2)
+    forward(5, 2)
+    accumulate_late(8)
+    finish_late((2, 3, 4))
+    forward(3, 3)
     attend(2)
-    forward(5, 2)
-    attend(3)
-    forward(3, 3)
-    attend(4)
-    attend(5)
     forward(4, 3)
-    attend(6)
+    finish_late((5, 6, 7))
     forward(6, 3)
     forward(5, 3)
+    attend(3)
+    attend(4)
+    forward(3, 4)
+    attend(5)
+    forward(4, 4)
+    attend(6)
+    forward(6, 4)
     attend(7)
-    forward(3, 4)
+    forward(5, 4)
     partial(1)
-    forward(4, 4)
-    forward(6, 4)
-    forward(5, 4)
+    forward(3, 5)
     partial(2)
-    for k in range(5, 9):
+    forward(4, 5)
+    forward(6, 5)
+    forward(5, 5)
+    forward(3, 6)
+    partial(3)
+    forward(4, 6)
+    relay(1)
+    forward(6, 6)
+    relay(2)
+    forward(5, 6)
+    partial(4)
+    for k in (7, 8):
+        forward(4, k)
+        partial(k - 2)
+        forward(6, k)
+        relay(k - 4)
         forward(3, k)
-        forward(4, k)
-        relay(k - 4)
-        forward(6, k)
         forward(5, k)
-        partial(k - 2)
     relay(5)
     partial(7)
     relay(6)
@@ -439,7 +459,7 @@
             vmem((8, SEQ, HEAD_DIM), bf16), vmem((SEQ, HEAD_DIM), bf16), vmem((SEQ, HEAD_DIM), bf16),
             vmem((SEQ, OE + OL), bf16), vmem((16, SEQ, 128), bf16), vmem((4, SEQ, 128), bf16),
             vmem((3, 4, SEQ, 128), bf16), vmem((7, 2, 256, 128), bf16),
-            dma((2,)), dma((1,)), dma((8,)), dma((1,)), dma((3,)), dma((7,)), dma((7, 15)),
+            dma((2,)), dma((1,)), dma((8,)), dma((1,)), dma((3,)), dma((7,)), dma((4, 15)),
             dma((2,)), dma((2, 9)), dma((1,)), dma((1,)), dma((1,)), dma((3, 4)), dma((7, 2)),
         ],
         compiler_params=pltpu.CompilerParams(

time: 108 us -> 106 us (0.981)
    pallas_call x1, Pallas kernels: 105 us -> 104 us  [body(): pl.pallas_call(kernel, out_shape=jax.ShapeDtypeStruct((SEQ, FEAT), bf16),...]
where the time goes in v3:
time: 106 us; the launch traced here: 105 us
  Pallas kernels  104 us (98%)
    pallas_call x1, Pallas kernels, body(): pl.pallas_call(kernel, out_shape=jax.ShapeDtypeStruct((SEQ, FEAT), bf16),...  104 us

profile of v3, /device:TPU:24, one launch (start us, length us, event | category | flops | bytes accessed | tf_op | source)
XLA Modules:
  0.0 104.7 jit_solution(6618054789419831342)
XLA Ops:
  0.0 103.9 %section.1 = bf16[512,512]{1,0:T(8,128)(2,1)S(1)} custom-call(bf16[512,512]{1,0:T(8,128)(2,1)} %bitcast.8, bf16[64,1024]{1,0:T(8,128)(2,1)} %bitcast.9, bf16[64,256]{1,0:T(8,128)(2,1)} %bitcast.11, bf16[64,1024]{1,0:T(8,128)(2,1)} %bitcast.10, f32[2,512,128]{2,1,0:T(8,128)} %constant.2.clone.table_hbm), custom_call_target="tpu_custom_call" | custom-call | tf_op jit(solution)/shard_map/section/pallas_call | solution.py:448
  103.9 0.8 copy.7

commit v4 on v3

--- a/solution.py
+++ b/solution.py
@@ -272,49 +272,49 @@
         j = lax.rem(owner + YN - t, YN) - 1
         remote(pb.at[slot], rb.at[j, quarter], ps.at[0], pr.at[j, quarter], (s, f, owner)).start()
 
-    def partial(k):
+    def partial(k, x):
+        pair = pair_of(k)
+        quarter = lax.rem(pair, 4)
+        b = pl.ds(x * ZN + 2 * pair, 2)
+        value = lax.dot_general(mx[:, 0:OE], oe[b].reshape(128, OE), NT, preferred_element_type=jnp.float32)
+        value = value + lax.dot_general(mx[:, OE:], ol[b].reshape(128, OL), NT, preferred_element_type=jnp.float32)
+        value = value.astype(jnp.bfloat16)
+        owner = 2 * x + pair // 4
+        slot = 2 * (k - 1) + x
+
+        @pl.when(owner == t)
+        def _():
+            po[pl.ds(quarter, 1)] = value[None]
+
+        @pl.when(owner != t)
+        def _():
+            pb[pl.ds(slot, 1)] = value[None]
+            if k == 8:
+                to_owner(k, slot, quarter, owner)
+
+        if k < 8:
+            @pl.when(owner == ydev(2))
+            def _():
+                for side in (0, 1):
+                    half = pb.at[slot, pl.ds(256 * side, 256)]
+                    remote(half, rl.at[k - 1, side], ps.at[0], rr.at[k - 1, side], (s, f, ydev(1 + 2 * side))).start()
+
+    def near(k):
+        partial(k, xh)
+
+    def far(k):
         if k == 1:
             xwait(1, 0)
         xwait(1, k)
+        partial(k, xo)
+
+    def relay(k, x):
         pair = pair_of(k)
-        quarter = lax.rem(pair, 4)
-
-        def weights(buf, width):
-            return jnp.concatenate([buf[pl.ds(x * ZN + 2 * pair, 2)].reshape(128, width) for x in (0, 1)], axis=0)
-
-        both = lax.dot_general(mx[:, 0:OE], weights(oe, OE), NT, preferred_element_type=jnp.float32)
-        both = both + lax.dot_general(mx[:, OE:], weights(ol, OL), NT, preferred_element_type=jnp.float32)
-        both = both.astype(jnp.bfloat16)
-        for x in (0, 1):
-            owner = 2 * x + pair // 4
-            slot = 2 * (k - 1) + x
-            value = both[:, 128 * x : 128 * x + 128]
-
-            @pl.when(owner == t)
+        owner = 2 * x + pair // 4
+        slot = 2 * (k - 1) + x
+        for side in (0, 1):
+            @pl.when(owner == ydev(1 + 2 * side))
             def _():
-                po[pl.ds(quarter, 1)] = value[None]
-
-            @pl.when(owner != t)
-            def _():
-                pb[slot] = value
-                if k == 8:
-                    to_owner(k, slot, quarter, owner)
-
-            if k < 8:
-                @pl.when(owner == ydev(2))
-                def _():
-                    for side in (0, 1):
-                        half = pb.at[slot, pl.ds(256 * side, 256)]
-                        remote(half, rl.at[k - 1, side], ps.at[0], rr.at[k - 1, side], (s, f, ydev(1 + 2 * side))).start()
-
-    def relay(k):
-        pair = pair_of(k)
-
-        @pl.when(pair // 4 != lax.rem(t, 2))
-        def _():
-            for side in (0, 1):
-                owner = ydev(1 + 2 * side)
-                slot = 2 * (k - 1) + owner // 2
                 dst = rl.at[k - 1, side]
                 remote(dst, dst, ps.at[0], rr.at[k - 1, side], (s, f, owner)).wait_recv()
                 rows = slice(256 * side, 256 * side + 256)
@@ -374,42 +374,62 @@
     forward(4, 3)
     finish_late((5, 6, 7))
     forward(6, 3)
+    attend(3)
     forward(5, 3)
-    attend(3)
     attend(4)
+    attend(5)
     forward(3, 4)
-    attend(5)
+    attend(6)
+    attend(7)
+    near(1)
     forward(4, 4)
-    attend(6)
+    far(1)
     forward(6, 4)
-    attend(7)
+    near(2)
     forward(5, 4)
-    partial(1)
+    far(2)
     forward(3, 5)
-    partial(2)
     forward(4, 5)
     forward(6, 5)
+    near(3)
     forward(5, 5)
+    relay(1, xh)
     forward(3, 6)
-    partial(3)
+    far(3)
+    relay(1, xo)
     forward(4, 6)
-    relay(1)
+    relay(2, xh)
     forward(6, 6)
-    relay(2)
+    near(4)
     forward(5, 6)
-    partial(4)
-    for k in (7, 8):
-        forward(4, k)
-        partial(k - 2)
-        forward(6, k)
-        relay(k - 4)
-        forward(3, k)
-        forward(5, k)
-    relay(5)
-    partial(7)
-    relay(6)
-    partial(8)
-    relay(7)
+    relay(2, xo)
+    forward(4, 7)
+    far(4)
+    relay(3, xh)
+    forward(6, 7)
+    near(5)
+    forward(3, 7)
+    relay(3, xo)
+    forward(5, 7)
+    forward(4, 8)
+    far(5)
+    relay(4, xh)
+    forward(6, 8)
+    near(6)
+    forward(3, 8)
+    relay(4, xo)
+    forward(5, 8)
+    near(7)
+    near(8)
+    far(6)
+    relay(5, xh)
+    relay(5, xo)
+    relay(6, xh)
+    far(7)
+    relay(7, xh)
+    relay(6, xo)
+    far(8)
+    relay(7, xo)
 
     for k in range(1, 9):
         pair = pair_of(k)

time: 106 us -> 106 us (level); the launches traced: 105 us -> 106 us
    pallas_call x1, Pallas kernels: 104 us -> 105 us  [body(): pl.pallas_call(kernel, out_shape=jax.ShapeDtypeStruct((SEQ, FEAT), bf16),...]
where the time goes in v4:
time: 106 us
  Pallas kernels  105 us (99%)
    pallas_call x1, Pallas kernels, body(): pl.pallas_call(kernel, out_shape=jax.ShapeDtypeStruct((SEQ, FEAT), bf16),...  105 us

profile of v4, /device:TPU:24, one launch (start us, length us, event | category | flops | bytes accessed | tf_op | source)
XLA Modules:
  0.0 106.1 jit_solution(8076667373893421542)
XLA Ops:
  0.0 105.3 %section.1 = bf16[512,512]{1,0:T(8,128)(2,1)S(1)} custom-call(bf16[512,512]{1,0:T(8,128)(2,1)} %bitcast.8, bf16[64,1024]{1,0:T(8,128)(2,1)} %bitcast.9, bf16[64,256]{1,0:T(8,128)(2,1)} %bitcast.11, bf16[64,1024]{1,0:T(8,128)(2,1)} %bitcast.10, f32[2,512,128]{2,1,0:T(8,128)} %constant.2.clone.table_hbm), custom_call_target="tpu_custom_call" | custom-call | tf_op jit(solution)/shard_map/section/pallas_call | solution.py:468
  105.3 0.8 copy.7
